TPU v7x, 512 devices: a whole 4x4x16 slice. The times are simulated.
512 devices in a mesh: depth: 8 (over y, core), lon: 64 (over x, z).
Axes of the slice: x: 4, y: 4, z: 16, core: 2. Of those that a mesh axis runs over, the one named last changes fastest.
Arguments:
- probes: float32 [16, 1179648], P(None, ('depth', 'lon'))
- coords: float32 [3, 1179648], P(None, ('depth', 'lon')), as said below
- pair_tiles: int32 [2, 57344], P(None, ('depth', 'lon')), may hold values from 0 to 42, as said below
- scales: float32 [2], replicated, may hold values from 0.5 to 2
Outputs:
- solution: float32 [16, 1179648], P(None, ('depth', 'lon'))
- residual: float32 [16, 1179648], P(None, ('depth', 'lon'))
Inputs may be any that keep to these rules, and one draw needn't show every extreme that they name: `pair_tiles`: row 0 holds row tiles 0 to 8 of the device holding the entry, used slots first, then 9 in every unused slot. Row 1 holds codes s * 9 + t of tile t of the same device (s = 0), of the device one lower (1) or one higher (2) along lon, one lower (3) or one higher (4) along depth; codes with s = 1 have t >= 7, codes with s = 2 have t < 2, codes with s = 3 or 4 have 2 <= t < 7; no code points past an edge of the mesh; unused slots hold code 0. `coords`: two points closer than 1 always lie in tiles that form a used pair.
All inputs are finite; a program needn't handle non-finite values.
Results may differ from a plain program's by a relative error of at most 0.0003.
Values sent between devices are 32-bit elements; how exact they have to be, the bound alone decides.
No kernel may reach another device: no remote copies, remote signals or barrier semaphores. Data moves between devices by JAX's collectives and lax.ppermute only.
A program may use at most 64 MiB of HBM per device.

v0:
```python
import jax
import jax.numpy as jnp
from jax import lax
from jax.sharding import PartitionSpec as P

PROBES = 16
TILE = 256
ITERS = 2


pair_block = 16


def padded(value, sides, width):
    for axis, dim in sides:
        count, length = (lax.axis_size(axis), value.shape[dim])
        up = [(i, (i + 1) % count) for i in range(count - 1)]
        down = [(j, i) for i, j in up]
        last = lax.slice_in_dim(value, length - width, length, axis=dim)
        leading = lax.slice_in_dim(value, 0, width, axis=dim)
        before = lax.ppermute(last, axis, up)
        after = lax.ppermute(leading, axis, down)
        value = jnp.concatenate([before, value, after], axis=dim)
    return value


def kernel_tile(near_pts, far_pts):
    dist_sq = (near_pts[0][:, :, None] - far_pts[0][:, None, :]) ** 2
    dist_sq = dist_sq + (near_pts[1][:, :, None] - far_pts[1][:, None, :]) ** 2
    dist_sq = dist_sq + (near_pts[2][:, :, None] - far_pts[2][:, None, :]) ** 2
    radius = jnp.sqrt(dist_sq)
    inside = jnp.maximum(1.0 - radius, 0.0)
    return inside**4 * (4.0 * radius + 1.0)


def inner_product(first_arr, second_arr):
    return jnp.sum(first_arr * second_arr, axis=(1, 2))


def squares_total(residual):
    return lax.psum(inner_product(residual, residual), ("depth", "lon"))


def body(probes, coords, pair_tiles, scales):
    tiles_here = probes.shape[1] // TILE
    own_dir = probes.reshape(PROBES, tiles_here, TILE)
    own_pts = coords.reshape(3, tiles_here, TILE)
    row_tiles = pair_tiles[0]
    col_codes = pair_tiles[1]
    band_first = 0
    live_pairs = jnp.sum((row_tiles < tiles_here).astype(jnp.int32))
    blocks = (live_pairs + pair_block - 1) // pair_block
    tile_range = jnp.arange(tiles_here, dtype=jnp.int32)

    def neighbour_tiles(stacked):
        lon_side = padded(stacked, (("lon", 1),), tiles_here)
        band_side = padded(stacked[None, :, band_first:tiles_here], (("depth", 0),), 1)
        return jnp.concatenate(
            [
                stacked,
                lon_side[:, :tiles_here],
                lon_side[:, tiles_here + tiles_here :],
                band_side[0],
                band_side[2],
            ],
            axis=1,
        )

    ext_first = neighbour_tiles(jnp.concatenate([own_pts, own_dir], axis=0))
    ext_pts = ext_first[:3]
    first_dir = ext_first[3:]
    solution = jnp.zeros(own_dir.shape, jnp.float32)
    residual = own_dir
    direction = own_dir
    norm_now = squares_total(residual)
    for sweep_index in range(ITERS):
        if sweep_index == 0:
            ext_dir = first_dir
        else:
            ext_dir = neighbour_tiles(direction)

        def add_block(block_index, running):
            first_pair = block_index * pair_block
            near_rows = lax.dynamic_slice_in_dim(row_tiles, first_pair, pair_block)
            far_rows = lax.dynamic_slice_in_dim(col_codes, first_pair, pair_block)
            near_pts = jnp.take(ext_pts, jnp.minimum(near_rows, tiles_here - 1), axis=1)
            far_pts = jnp.take(ext_pts, far_rows, axis=1)
            far_dir = jnp.take(ext_dir, far_rows, axis=1)
            weights = kernel_tile(near_pts, far_pts)
            contrib = jnp.einsum("pij,cpj->cpi", weights, far_dir, precision=lax.Precision.HIGHEST)
            placing = (near_rows[:, None] == tile_range[None, :]).astype(jnp.float32)
            return running + jnp.einsum(
                "cpi,pt->cti", contrib, placing, precision=lax.Precision.HIGHEST
            )

        running = lax.fori_loop(0, blocks, add_block, jnp.zeros(direction.shape, jnp.float32))
        applied = scales[1] * direction + scales[0] * running
        curvature = lax.psum(inner_product(direction, applied), ("depth", "lon"))
        step_size = norm_now / curvature
        solution = solution + step_size[:, None, None] * direction
        residual = residual - step_size[:, None, None] * applied
        norm_next = squares_total(residual)
        direction = residual + (norm_next / norm_now)[:, None, None] * direction
        norm_now = norm_next
    return (
        solution.reshape(PROBES, tiles_here * TILE),
        residual.reshape(PROBES, tiles_here * TILE),
    )


def solution(mesh):
    return jax.shard_map(
        body,
        mesh=mesh,
        in_specs=(
            P(None, ("depth", "lon")),
            P(None, ("depth", "lon")),
            P(None, ("depth", "lon")),
            P(),
        ),
        out_specs=(P(None, ("depth", "lon")), P(None, ("depth", "lon"))),
        check_vma=False,
    )
```

profile of v0, /device:TPU:1, one launch (start us, length us, event | category | flops | bytes accessed | tf_op | source)
XLA Modules:
  0.0 507.7 jit_solution(1348659020692717885)
XLA Ops:
  0.7 1.0 reshape.45
  1.7 0.8 reshape.46
  2.5 4.6 collective-permute-start.2
  7.1 5.5 %collective-permute-start.3 = (f32[1,19,9,256]{3,2,1,0:T(8,128)S(1)}, f32[1,19,9,256]{3,2,1,0:T(8,128)S(1)}, u32[]{:S(2)}, u32[]{:S(2)}) collective-permute-start(f32[1,19,9,256]{3,2,1,0:T(8,128)S(1)} %bitcast.141), channel_id=1, source_target_pairs={{64,0},{128,64},{192,128},{256,192},{320,256},{384,320},{448,384},... | collective-permute-start | bytes 525320 | tf_op jit(solution)/shard_map/ppermute | solution.py:22
  12.6 1.3 collective-permute-start
  13.9 1.3 collective-permute-start.1
  15.2 0.6 fusion.84
  16.7 0.7 fusion.89
  17.4 3.3 collective-permute-done
  20.6 4.3 collective-permute-done.1
  24.9 1.6 concatenate.10
  27.1 72.6 %while.22 = (s32[]{:T(128)}, f32[16,9,256]{2,1,0:T(8,128)S(1)}, s32[]{:T(128)}, s32[112]{0:T(128)S(1)}, s32[112]{0:T(128)S(1)}, /*index=5*/f32[16,45,256]{2,0,1:...) while((s32[]{:T(128)}, f32[16,9,256]{2,1,0:T(8,128)S(1)}, ...), condition=%wide.region_4.0_spmd.clone, body=%wide.region_3.6_spmd.clone.sunk | while | flops 224262496 | bytes 2499503 | solution.py:96
  27.3 0.6 gather_fusion
  28.0 0.6 gather_fusion.1
  29.4 7.7 %fusion.112 = f32[16,16,256]{2,1,0:T(8,128)S(1)} fusion(f32[16,256]{1,0:T(8,128)S(1)} %bitcast.142, f32[16,256]{1,0:T(8,128)S(1)} %bitcast.148, f32[16,256]{1,0:T(8,128)S(1)} %bitcast.144, f32[16,256]{1,0:T(8,128)S(1)} %bitcast.150, f32[16,256]{1,0:T(8,128)S(1)} %bitcast.146, f32[16,256]{1,0:T(8,128)S(1)} %bitcast.152, ...), kind=kOutput, calls=%fused_computation.8.clone.1 | convolution fusion | flops 217120768 | bytes 622608 | tf_op jit(solution)/shard_map/while/body/pij,cpj->cpi/dot_general | solution.py:90
  37.6 0.6 gather_fusion
  39.8 7.7 %fusion.112 = f32[16,16,256]{2,1,0:T(8,128)S(1)} fusion(f32[16,256]{1,0:T(8,128)S(1)} %bitcast.142, f32[16,256]{1,0:T(8,128)S(1)} %bitcast.148, f32[16,256]{1,0:T(8,128)S(1)} %bitcast.144, f32[16,256]{1,0:T(8,128)S(1)} %bitcast.150, f32[16,256]{1,0:T(8,128)S(1)} %bitcast.146, f32[16,256]{1,0:T(8,128)S(1)} %bitcast.152, ...), kind=kOutput, calls=%fused_computation.8.clone.1 | convolution fusion | flops 217120768 | bytes 622608 | tf_op jit(solution)/shard_map/while/body/pij,cpj->cpi/dot_general | solution.py:90
  48.0 0.6 gather_fusion
  50.1 7.7 %fusion.112 = f32[16,16,256]{2,1,0:T(8,128)S(1)} fusion(f32[16,256]{1,0:T(8,128)S(1)} %bitcast.142, f32[16,256]{1,0:T(8,128)S(1)} %bitcast.148, f32[16,256]{1,0:T(8,128)S(1)} %bitcast.144, f32[16,256]{1,0:T(8,128)S(1)} %bitcast.150, f32[16,256]{1,0:T(8,128)S(1)} %bitcast.146, f32[16,256]{1,0:T(8,128)S(1)} %bitcast.152, ...), kind=kOutput, calls=%fused_computation.8.clone.1 | convolution fusion | flops 217120768 | bytes 622608 | tf_op jit(solution)/shard_map/while/body/pij,cpj->cpi/dot_general | solution.py:90
  58.4 0.6 gather_fusion
  59.1 0.6 gather_fusion.1
  60.5 7.7 %fusion.112 = f32[16,16,256]{2,1,0:T(8,128)S(1)} fusion(f32[16,256]{1,0:T(8,128)S(1)} %bitcast.142, f32[16,256]{1,0:T(8,128)S(1)} %bitcast.148, f32[16,256]{1,0:T(8,128)S(1)} %bitcast.144, f32[16,256]{1,0:T(8,128)S(1)} %bitcast.150, f32[16,256]{1,0:T(8,128)S(1)} %bitcast.146, f32[16,256]{1,0:T(8,128)S(1)} %bitcast.152, ...), kind=kOutput, calls=%fused_computation.8.clone.1 | convolution fusion | flops 217120768 | bytes 622608 | tf_op jit(solution)/shard_map/while/body/pij,cpj->cpi/dot_general | solution.py:90
  68.7 0.6 gather_fusion
  69.5 0.6 gather_fusion.1
  70.9 7.7 %fusion.112 = f32[16,16,256]{2,1,0:T(8,128)S(1)} fusion(f32[16,256]{1,0:T(8,128)S(1)} %bitcast.142, f32[16,256]{1,0:T(8,128)S(1)} %bitcast.148, f32[16,256]{1,0:T(8,128)S(1)} %bitcast.144, f32[16,256]{1,0:T(8,128)S(1)} %bitcast.150, f32[16,256]{1,0:T(8,128)S(1)} %bitcast.146, f32[16,256]{1,0:T(8,128)S(1)} %bitcast.152, ...), kind=kOutput, calls=%fused_computation.8.clone.1 | convolution fusion | flops 217120768 | bytes 622608 | tf_op jit(solution)/shard_map/while/body/pij,cpj->cpi/dot_general | solution.py:90
  79.1 0.6 gather_fusion
  81.2 7.7 %fusion.112 = f32[16,16,256]{2,1,0:T(8,128)S(1)} fusion(f32[16,256]{1,0:T(8,128)S(1)} %bitcast.142, f32[16,256]{1,0:T(8,128)S(1)} %bitcast.148, f32[16,256]{1,0:T(8,128)S(1)} %bitcast.144, f32[16,256]{1,0:T(8,128)S(1)} %bitcast.150, f32[16,256]{1,0:T(8,128)S(1)} %bitcast.146, f32[16,256]{1,0:T(8,128)S(1)} %bitcast.152, ...), kind=kOutput, calls=%fused_computation.8.clone.1 | convolution fusion | flops 217120768 | bytes 622608 | tf_op jit(solution)/shard_map/while/body/pij,cpj->cpi/dot_general | solution.py:90
  90.3 0.6 gather_fusion.1
  91.6 7.7 %fusion.112 = f32[16,16,256]{2,1,0:T(8,128)S(1)} fusion(f32[16,256]{1,0:T(8,128)S(1)} %bitcast.142, f32[16,256]{1,0:T(8,128)S(1)} %bitcast.148, f32[16,256]{1,0:T(8,128)S(1)} %bitcast.144, f32[16,256]{1,0:T(8,128)S(1)} %bitcast.150, f32[16,256]{1,0:T(8,128)S(1)} %bitcast.146, f32[16,256]{1,0:T(8,128)S(1)} %bitcast.152, ...), kind=kOutput, calls=%fused_computation.8.clone.1 | convolution fusion | flops 217120768 | bytes 622608 | tf_op jit(solution)/shard_map/while/body/pij,cpj->cpi/dot_general | solution.py:90
  99.7 1.5 multiply_reduce_fusion.2
  101.2 106.6 %all-reduce = (f32[16]{0:T(128)S(1)}, f32[16]{0:T(128)S(1)}) all-reduce(f32[16]{0:T(128)S(1)} %multiply_reduce_fusion.3, f32[16]{0:T(128)S(1)} %multiply_reduce_fusion.2), channel_id=1, replica_groups=mesh['depth'=8,'lon'=64] {'depth','lon'}, use_global_device_ids=true, to_apply=%region_1.2 | all-reduce | flops 32 | bytes 256 | tf_op jit(solution)/shard_map/psum | solution.py:41
  207.8 1.5 multiply_reduce_fusion.1
  209.3 98.5 %psum.30 = f32[16]{0:T(128)S(1)} all-reduce(f32[16]{0:T(128)S(1)} %multiply_reduce_fusion.1), channel_id=1, replica_groups=mesh['depth'=8,'lon'=64] {'depth','lon'}, use_global_device_ids=true, to_apply=%region_8.11 | all-reduce | flops 16 | bytes 128 | tf_op jit(solution)/shard_map/psum | solution.py:41
  307.8 1.4 multiply_add_fusion.2
  309.2 2.9 collective-permute-start.6
  312.1 1.9 collective-permute-start.7
  314.0 3.7 collective-permute-start.4
  317.7 1.3 collective-permute-start.5
  319.1 0.7 collective-permute-done.7
  319.8 3.4 collective-permute-done.4
  323.2 4.1 collective-permute-done.5
  327.3 1.2 concatenate.11
  328.9 72.6 %while.23 = (s32[]{:T(128)}, f32[16,9,256]{2,1,0:T(8,128)S(1)}, s32[]{:T(128)}, s32[112]{0:T(128)S(1)}, s32[112]{0:T(128)S(1)}, /*index=5*/f32[16,45,256]{2,0,1:...) while((s32[]{:T(128)}, f32[16,9,256]{2,1,0:T(8,128)S(1)}, ...), condition=%wide.region_10.13_spmd.clone, body=%wide.region_9.12_spmd.clone.sunk | while | flops 224262496 | bytes 2499503 | solution.py:96
  329.1 0.6 gather_fusion.3
  329.8 0.6 gather_fusion.4
  331.2 7.7 %fusion.120 = f32[16,16,256]{2,1,0:T(8,128)S(1)} fusion(f32[16,256]{1,0:T(8,128)S(1)} %bitcast.143, f32[16,256]{1,0:T(8,128)S(1)} %bitcast.149, f32[16,256]{1,0:T(8,128)S(1)} %bitcast.145, f32[16,256]{1,0:T(8,128)S(1)} %bitcast.151, f32[16,256]{1,0:T(8,128)S(1)} %bitcast.147, f32[16,256]{1,0:T(8,128)S(1)} %bitcast.153, ...), kind=kOutput, calls=%fused_computation.63.clone.1 | convolution fusion | flops 217120768 | bytes 622608 | tf_op jit(solution)/shard_map/while/body/pij,cpj->cpi/dot_general | solution.py:90
  339.4 0.6 gather_fusion.3
  341.6 7.7 %fusion.120 = f32[16,16,256]{2,1,0:T(8,128)S(1)} fusion(f32[16,256]{1,0:T(8,128)S(1)} %bitcast.143, f32[16,256]{1,0:T(8,128)S(1)} %bitcast.149, f32[16,256]{1,0:T(8,128)S(1)} %bitcast.145, f32[16,256]{1,0:T(8,128)S(1)} %bitcast.151, f32[16,256]{1,0:T(8,128)S(1)} %bitcast.147, f32[16,256]{1,0:T(8,128)S(1)} %bitcast.153, ...), kind=kOutput, calls=%fused_computation.63.clone.1 | convolution fusion | flops 217120768 | bytes 622608 | tf_op jit(solution)/shard_map/while/body/pij,cpj->cpi/dot_general | solution.py:90
  349.8 0.6 gather_fusion.3
  351.9 7.7 %fusion.120 = f32[16,16,256]{2,1,0:T(8,128)S(1)} fusion(f32[16,256]{1,0:T(8,128)S(1)} %bitcast.143, f32[16,256]{1,0:T(8,128)S(1)} %bitcast.149, f32[16,256]{1,0:T(8,128)S(1)} %bitcast.145, f32[16,256]{1,0:T(8,128)S(1)} %bitcast.151, f32[16,256]{1,0:T(8,128)S(1)} %bitcast.147, f32[16,256]{1,0:T(8,128)S(1)} %bitcast.153, ...), kind=kOutput, calls=%fused_computation.63.clone.1 | convolution fusion | flops 217120768 | bytes 622608 | tf_op jit(solution)/shard_map/while/body/pij,cpj->cpi/dot_general | solution.py:90
  360.9 0.6 gather_fusion.4
  362.3 7.7 %fusion.120 = f32[16,16,256]{2,1,0:T(8,128)S(1)} fusion(f32[16,256]{1,0:T(8,128)S(1)} %bitcast.143, f32[16,256]{1,0:T(8,128)S(1)} %bitcast.149, f32[16,256]{1,0:T(8,128)S(1)} %bitcast.145, f32[16,256]{1,0:T(8,128)S(1)} %bitcast.151, f32[16,256]{1,0:T(8,128)S(1)} %bitcast.147, f32[16,256]{1,0:T(8,128)S(1)} %bitcast.153, ...), kind=kOutput, calls=%fused_computation.63.clone.1 | convolution fusion | flops 217120768 | bytes 622608 | tf_op jit(solution)/shard_map/while/body/pij,cpj->cpi/dot_general | solution.py:90
  370.5 0.6 gather_fusion.3
  371.3 0.6 gather_fusion.4
  372.7 7.7 %fusion.120 = f32[16,16,256]{2,1,0:T(8,128)S(1)} fusion(f32[16,256]{1,0:T(8,128)S(1)} %bitcast.143, f32[16,256]{1,0:T(8,128)S(1)} %bitcast.149, f32[16,256]{1,0:T(8,128)S(1)} %bitcast.145, f32[16,256]{1,0:T(8,128)S(1)} %bitcast.151, f32[16,256]{1,0:T(8,128)S(1)} %bitcast.147, f32[16,256]{1,0:T(8,128)S(1)} %bitcast.153, ...), kind=kOutput, calls=%fused_computation.63.clone.1 | convolution fusion | flops 217120768 | bytes 622608 | tf_op jit(solution)/shard_map/while/body/pij,cpj->cpi/dot_general | solution.py:90
  380.9 0.6 gather_fusion.3
  383.0 7.7 %fusion.120 = f32[16,16,256]{2,1,0:T(8,128)S(1)} fusion(f32[16,256]{1,0:T(8,128)S(1)} %bitcast.143, f32[16,256]{1,0:T(8,128)S(1)} %bitcast.149, f32[16,256]{1,0:T(8,128)S(1)} %bitcast.145, f32[16,256]{1,0:T(8,128)S(1)} %bitcast.151, f32[16,256]{1,0:T(8,128)S(1)} %bitcast.147, f32[16,256]{1,0:T(8,128)S(1)} %bitcast.153, ...), kind=kOutput, calls=%fused_computation.63.clone.1 | convolution fusion | flops 217120768 | bytes 622608 | tf_op jit(solution)/shard_map/while/body/pij,cpj->cpi/dot_general | solution.py:90
  392.0 0.6 gather_fusion.4
  393.4 7.7 %fusion.120 = f32[16,16,256]{2,1,0:T(8,128)S(1)} fusion(f32[16,256]{1,0:T(8,128)S(1)} %bitcast.143, f32[16,256]{1,0:T(8,128)S(1)} %bitcast.149, f32[16,256]{1,0:T(8,128)S(1)} %bitcast.145, f32[16,256]{1,0:T(8,128)S(1)} %bitcast.151, f32[16,256]{1,0:T(8,128)S(1)} %bitcast.147, f32[16,256]{1,0:T(8,128)S(1)} %bitcast.153, ...), kind=kOutput, calls=%fused_computation.63.clone.1 | convolution fusion | flops 217120768 | bytes 622608 | tf_op jit(solution)/shard_map/while/body/pij,cpj->cpi/dot_general | solution.py:90
  401.5 1.5 multiply_reduce_fusion
  403.0 101.8 %psum.31 = f32[16]{0:T(128)S(1)} all-reduce(f32[16]{0:T(128)S(1)} %multiply_reduce_fusion), channel_id=1, replica_groups=mesh['depth'=8,'lon'=64] {'depth','lon'}, use_global_device_ids=true, to_apply=%region_12.15 | all-reduce | flops 16 | bytes 128 | tf_op jit(solution)/shard_map/psum | solution.py:98
  504.8 1.4 multiply_subtract_fusion
  506.2 0.8 copy.24
  507.0 0.8 copy.25
  (242 shorter events, 25.9 us)
Async XLA Ops:
  0.6 15.9 %copy-start = (f32[16,2304]{1,0:T(8,128)S(1)}, f32[16,2304]{1,0:T(8,128)}, u32[]{:S(2)}) copy-start(f32[16,2304]{1,0:T(8,128)} %param.12) | copy-start | bytes 442372
  0.6 14.6 %copy-start.2 = (s32[2,112]{1,0:T(2,128)S(1)}, s32[2,112]{1,0:T(2,128)}, u32[]{:S(2)}) copy-start(s32[2,112]{1,0:T(2,128)} %param.14) | copy-start | bytes 2692
  0.6 16.0 %copy-start.1 = (f32[2]{0:T(128)S(1)}, f32[2]{0:T(128)}, u32[]{:S(2)}) copy-start(f32[2]{0:T(128)} %param.15) | copy-start | bytes 28
  2.5 14.9 %collective-permute-start.2 = (f32[1,19,9,256]{3,2,1,0:T(8,128)S(1)}, f32[1,19,9,256]{3,2,1,0:T(8,128)S(1)}, u32[]{:S(2)}, u32[]{:S(2)}) collective-permute-start(f32[1,19,9,256]{3,2,1,0:T(8,128)S(1)} %bitcast.140), channel_id=1, source_target_pairs={{0,64},{64,128},{128,192},{192,256},{256,320},{320,384},{384,448},... | collective-permute-start | bytes 525320 | tf_op jit(solution)/shard_map/ppermute | solution.py:21
  7.1 10.3 %collective-permute-start.3 = (f32[1,19,9,256]{3,2,1,0:T(8,128)S(1)}, f32[1,19,9,256]{3,2,1,0:T(8,128)S(1)}, u32[]{:S(2)}, u32[]{:S(2)}) collective-permute-start(f32[1,19,9,256]{3,2,1,0:T(8,128)S(1)} %bitcast.141), channel_id=1, source_target_pairs={{64,0},{128,64},{192,128},{256,192},{320,256},{384,320},{448,384},... | collective-permute-start | bytes 525320 | tf_op jit(solution)/shard_map/ppermute | solution.py:22
  12.6 8.0 %collective-permute-start = (f32[19,9,256]{2,1,0:T(8,128)S(1)}, f32[19,9,256]{2,1,0:T(8,128)S(1)}, u32[]{:S(2)}, u32[]{:S(2)}) collective-permute-start(f32[19,9,256]{2,1,0:T(8,128)S(1)} %constant_dynamic-update-slice_fusion), channel_id=1, source_target_pairs={{0,1},{1,2},{2,3},{3,4},{4,5},{5,6},{6,7},{7,8},{8,9},{9,10},{10,1... | collective-permute-start | bytes 525320 | tf_op jit(solution)/shard_map/ppermute | solution.py:21
  13.9 11.0 %collective-permute-start.1 = (f32[19,9,256]{2,1,0:T(8,128)S(1)}, f32[19,9,256]{2,1,0:T(8,128)S(1)}, u32[]{:S(2)}, u32[]{:S(2)}) collective-permute-start(f32[19,9,256]{2,1,0:T(8,128)S(1)} %constant_dynamic-update-slice_fusion), channel_id=1, source_target_pairs={{1,0},{2,1},{3,2},{4,3},{5,4},{6,5},{7,6},{8,7},{9,8},{10,9},{11,1... | collective-permute-start | bytes 525320 | tf_op jit(solution)/shard_map/ppermute | solution.py:22
  309.2 9.9 %collective-permute-start.6 = (f32[1,16,9,256]{3,2,1,0:T(8,128)S(1)}, f32[1,16,9,256]{3,2,1,0:T(8,128)S(1)}, u32[]{:S(2)}, u32[]{:S(2)}) collective-permute-start(f32[1,16,9,256]{3,2,1,0:T(8,128)S(1)} %bitcast.136), channel_id=1, source_target_pairs={{0,64},{64,128},{128,192},{192,256},{256,320},{320,384},{384,448},... | collective-permute-start | bytes 442376 | tf_op jit(solution)/shard_map/ppermute | solution.py:21
  312.1 7.7 %collective-permute-start.7 = (f32[1,16,9,256]{3,2,1,0:T(8,128)S(1)}, f32[1,16,9,256]{3,2,1,0:T(8,128)S(1)}, u32[]{:S(2)}, u32[]{:S(2)}) collective-permute-start(f32[1,16,9,256]{3,2,1,0:T(8,128)S(1)} %bitcast.137), channel_id=1, source_target_pairs={{64,0},{128,64},{192,128},{256,192},{320,256},{384,320},{448,384},... | collective-permute-start | bytes 442376 | tf_op jit(solution)/shard_map/ppermute | solution.py:22
  314.0 9.1 %collective-permute-start.4 = (f32[16,9,256]{2,1,0:T(8,128)S(1)}, f32[16,9,256]{2,1,0:T(8,128)S(1)}, u32[]{:S(2)}, u32[]{:S(2)}) collective-permute-start(f32[16,9,256]{2,1,0:T(8,128)S(1)} %multiply_add_fusion.2), channel_id=1, source_target_pairs={{0,1},{1,2},{2,3},{3,4},{4,5},{5,6},{6,7},{7,8},{8,9},{9,10},{10,1... | collective-permute-start | bytes 442376 | tf_op jit(solution)/shard_map/ppermute | solution.py:21
  317.7 9.5 %collective-permute-start.5 = (f32[16,9,256]{2,1,0:T(8,128)S(1)}, f32[16,9,256]{2,1,0:T(8,128)S(1)}, u32[]{:S(2)}, u32[]{:S(2)}) collective-permute-start(f32[16,9,256]{2,1,0:T(8,128)S(1)} %multiply_add_fusion.2), channel_id=1, source_target_pairs={{1,0},{2,1},{3,2},{4,3},{5,4},{6,5},{7,6},{8,7},{9,8},{10,9},{11,1... | collective-permute-start | bytes 442376 | tf_op jit(solution)/shard_map/ppermute | solution.py:22
where the time goes:
time: 509 us; the launch traced here: 508 us
  blocking collectives  307 us (60%)
  matrix products  114 us (22%)
  local copies, waits for them, and re-layouts  33.7 us (7%)
  starting transfers between devices  22.5 us (4%)
  waiting for transfers between devices  15.7 us (3%)
  other arithmetic  11.7 us (2%)
    psum x2, blocking collectives, squares_total(): return lax.psum(inner_product(residual, residual), ('depth', 'lon'))  205 us
    dot_general x14, matrix products, add_block(): jnp.einsum('pij,cpj->cpi', weights, far_dir, precision=lax.Precision.HIGH...  107 us
    psum x1, blocking collectives, body(): curvature = lax.psum(inner_product(direction, applied), ('depth', 'lon'))  102 us
    ppermute x4, starting transfers between devices, padded(): before = lax.ppermute(last, axis, up)  12.5 us
  transfers between devices with their start and end apart: 8, of which 5 were waited for; matrix products, arithmetic and copies ran while one was open for 0% of the time, Pallas kernels for 0%

commit v1 on v0

v1 whole, which is shorter than its diff:
```python
import jax
import jax.numpy as jnp
from jax import lax
from jax.experimental import pallas as pl
from jax.experimental.pallas import tpu as pltpu
from jax.sharding import Mesh, PartitionSpec as P

PROBES = 16
TILE = 256
TD = 9
BT = 2
MID = TD - 2 * BT
HALO = 2 * BT + 2 * MID
CHUNK = 32
ROWS = 24
FIRST = ROWS - PROBES
VMEM = pltpu.MemorySpace.VMEM
SMEM = pltpu.MemorySpace.SMEM
PARTS = ((0, BT), (BT, MID), (TD - BT, BT))


def call(kernel, out_shape, in_specs, scratch=(), aliases=None, flops=0, nbytes=0, limit=20):
    return pl.pallas_call(
        kernel,
        out_shape=out_shape,
        in_specs=in_specs,
        out_specs=jax.tree.map(lambda _: pl.BlockSpec(memory_space=VMEM), out_shape),
        scratch_shapes=scratch,
        input_output_aliases=aliases or {},
        compiler_params=pltpu.CompilerParams(vmem_limit_bytes=limit << 20),
        cost_estimate=pl.CostEstimate(flops=flops, bytes_accessed=nbytes, transcendentals=0),
    )


def spec(space=VMEM):
    return pl.BlockSpec(memory_space=space)


def f32(*shape):
    return jax.ShapeDtypeStruct(shape, jnp.float32)


def pack_kernel(probes, coords, left, mid, right):
    for (first, count), out in zip(PARTS, (left, mid, right)):
        cols = pl.ds(first * TILE, count * TILE)
        out[0:FIRST, :] = jnp.zeros((FIRST, count * TILE), jnp.float32)
        out[0:3, :] = coords[:, cols]
        out[FIRST:ROWS, :] = probes[:, cols]


def make_lists(pairs, slots, own, rows, cols):
    def step(j, counts):
        taken, inside = counts
        row, code = pairs[0, j], pairs[1, j]
        used = row < TD
        local = used & (code < TD)
        source = code // TD
        tile = code - source * TD
        if own:
            keep, place = local, tile
        else:
            keep = used & (code >= TD)
            place = jnp.where(
                source == 1,
                tile - (TD - BT),
                jnp.where(source == 2, tile + BT, tile + BT + jnp.where(source == 3, 0, MID)),
            )
        rows[taken] = row
        cols[taken] = place
        return taken + keep.astype(jnp.int32), inside + local.astype(jnp.int32)

    taken, inside = lax.fori_loop(0, slots, step, (0, 0))
    rows[taken] = 0
    cols[taken] = 0
    return taken, inside


def split(values):
    high = values.astype(jnp.bfloat16)
    return high, (values - high.astype(jnp.float32)).astype(jnp.bfloat16)


def put_vectors(values, vecs, at):
    high, low = split(values)
    vecs[at, 0:PROBES, :] = high
    vecs[at, PROBES:, :] = low


def evaluate(near, far, slot, high, low):
    x, y, z = near[0:1, :], near[1:2, :], near[2:3, :]
    for first in range(0, TILE, CHUNK):
        rows = pl.ds(first, CHUNK)
        dx = far[rows, 0:1] - x
        dy = far[rows, 1:2] - y
        dz = far[rows, 2:3] - z
        dist_sq = dx * dx + dy * dy + dz * dz
        radius = dist_sq * lax.rsqrt(jnp.maximum(dist_sq, 1e-30))
        inside = jnp.maximum(1.0 - radius, 0.0)
        square = inside * inside
        phi = (square * square) * (1.25 - inside)
        top, rest = split(phi)
        high[slot, rows, :] = top
        low[slot, rows, :] = rest


def multiply(vecs, source, slot, high, low):
    both = jnp.dot(vecs[source], high[slot], preferred_element_type=jnp.float32)
    rest = jnp.dot(vecs[source, 0:PROBES, :], low[slot], preferred_element_type=jnp.float32)
    return both[0:PROBES] + both[PROBES:] + rest


def first_sweep(base, taken, rows, cols, near, far, vecs, total, high, low):
    def phi(k):
        evaluate(near.at[rows[k]], far.at[cols[k]], base + k, high, low)

    @pl.when(taken > 0)
    def _():
        phi(0)

    def step(k, carry):
        a, b = rows[k - 1], cols[k - 1]
        total[a] += multiply(vecs, b, base + k - 1, high, low)
        phi(k)
        return carry

    lax.fori_loop(1, taken + 1, step, 0)


def second_sweep(base, taken, rows, cols, vecs, total, high, low):
    def step(k, carry):
        a, b = rows[k], cols[k]
        total[a] += multiply(vecs, b, base + k, high, low)
        return carry

    lax.fori_loop(0, taken, step, 0)


def own_blocks(refs):
    for (first, count), ref in zip(PARTS, refs):
        for t in range(count):
            yield first + t, ref, pl.ds(t * TILE, TILE)


def halo_blocks(from_left, from_right, below, above):
    at = 0
    for ref, count in ((from_left, BT), (from_right, BT), (below, MID), (above, MID)):
        for t in range(count):
            yield at, ref, pl.ds(t * TILE, TILE)
            at += 1


def phi_own_kernel(pairs, left, mid, right, total, high, low, rows, cols, near, far, vecs):
    taken, _ = make_lists(pairs, pairs.shape[1], True, rows, cols)
    for t, ref, at in own_blocks((left, mid, right)):
        near[t] = ref[0:FIRST, at]
        far[t] = ref[0:FIRST, at].T
        put_vectors(ref[FIRST:ROWS, at], vecs, t)
    total[...] = jnp.zeros_like(total)
    first_sweep(0, taken, rows, cols, near, far, vecs, total, high, low)


def phi_halo_kernel(
    pairs, scales, left, mid, right, from_left, from_right, below, above, part, high_in, low_in,
    p_left, p_mid, p_right, high, low, rows, cols, near, far, vecs, total,
):
    taken, base = make_lists(pairs, pairs.shape[1], False, rows, cols)
    for t, ref, at in own_blocks((left, mid, right)):
        near[t] = ref[0:FIRST, at]
    for t, ref, at in halo_blocks(from_left, from_right, below, above):
        far[t] = ref[0:FIRST, at].T
        put_vectors(ref[FIRST:ROWS, at], vecs, t)
    total[...] = part[...]
    first_sweep(base, taken, rows, cols, near, far, vecs, total, high, low)
    outs = {}
    for t, ref, at in own_blocks((p_left, p_mid, p_right)):
        outs[t] = (ref, at)
    for t, ref, at in own_blocks((left, mid, right)):
        out, place = outs[t]
        out[:, place] = scales[0] * (4.0 * total[t] - ref[FIRST:ROWS, at])


def own_kernel(pairs, left, mid, right, high, low, total, rows, cols, vecs):
    taken, _ = make_lists(pairs, pairs.shape[1], True, rows, cols)
    for t, ref, at in own_blocks((left, mid, right)):
        put_vectors(ref[:, at], vecs, t)
    total[...] = jnp.zeros_like(total)
    second_sweep(0, taken, rows, cols, vecs, total, high, low)


def halo_kernel(
    pairs, scales, probes, left, mid, right, from_left, from_right, below, above, part, high, low,
    image, dots, rows, cols, vecs, total,
):
    taken, base = make_lists(pairs, pairs.shape[1], False, rows, cols)
    for t, ref, at in halo_blocks(from_left, from_right, below, above):
        put_vectors(ref[:, at], vecs, t)
    total[...] = part[...]
    second_sweep(base, taken, rows, cols, vecs, total, high, low)
    sums = [jnp.zeros((PROBES, TILE), jnp.float32) for _ in range(5)]
    for t, ref, at in own_blocks((left, mid, right)):
        p = ref[:, at]
        u = scales[0] * (4.0 * total[t] - p)
        r = probes[:, pl.ds(t * TILE, TILE)]
        image[:, pl.ds(t * TILE, TILE)] = u
        for i, (one, other) in enumerate(((r, r), (r, p), (p, p), (r, u), (p, u))):
            sums[i] = sums[i] + one * other
    lane = lax.broadcasted_iota(jnp.int32, (PROBES, 128), 1)
    probe = lax.broadcasted_iota(jnp.int32, (PROBES, 128), 0)
    line = jnp.zeros((PROBES, 128), jnp.float32)
    for i, value in enumerate(sums):
        line = line + jnp.where(lane == i * PROBES + probe, jnp.sum(value, axis=1, keepdims=True), 0.0)
    dots[...] = jnp.broadcast_to(jnp.sum(line, axis=0, keepdims=True), dots.shape)


def pass_kernel(gathered, out):
    out[...] = jnp.broadcast_to(jnp.sum(gathered[...], axis=0, keepdims=True), out.shape)


def final_kernel(gathered, scales, probes, left, mid, right, image, solution, residual):
    line = jnp.sum(gathered[...], axis=0, keepdims=True)
    lane = lax.broadcasted_iota(jnp.int32, (PROBES, 128), 1)
    probe = lax.broadcasted_iota(jnp.int32, (PROBES, 128), 0)
    spread = jnp.broadcast_to(line, (PROBES, 128))
    rr, rp, pp, ru, pu = [
        jnp.sum(jnp.where(lane == i * PROBES + probe, spread, 0.0), axis=1, keepdims=True)
        for i in range(5)
    ]
    shift = scales[0] + scales[1]
    first = rr / (shift * rr + rp)
    ratio = rp / rr
    norm = first * first * (pp - rp * ratio)
    turn = norm / rr
    keep = first * ratio + turn
    curve = (
        shift * (norm + turn * norm) + keep * keep * rp - keep * first * (ru + pp) + first * first * pu
    )
    second = norm / curve
    own_r = first + second * keep
    own_p = second * first
    res_r = first * ratio - second * shift * keep
    res_p = second * (shift * first - keep) - first
    res_u = second * first
    for t, ref, at in own_blocks((left, mid, right)):
        cols = pl.ds(t * TILE, TILE)
        r, p = probes[:, cols], ref[:, at]
        solution[:, cols] = own_r * r - own_p * p
        residual[:, cols] = res_r * r + res_p * p + res_u * image[:, cols]


def body(probes, coords, pairs, scales):
    slots = pairs.shape[1]
    width = probes.shape[1]
    lists = [pltpu.SMEM((slots + 1,), jnp.int32), pltpu.SMEM((slots + 1,), jnp.int32)]
    pair_flops = 40 * TILE * TILE * slots // 2
    stored = (slots + 1, TILE, TILE)
    kept = (pltpu.VMEM(stored, jnp.bfloat16), pltpu.VMEM(stored, jnp.bfloat16))
    pieces = lambda rows: tuple(f32(rows, count * TILE) for _, count in PARTS)

    def exchange(left, mid, right):
        lon = ("x", "z")
        depth = ("y", "core")
        up = lambda axes: [(i, i + 1) for i in range(lax.axis_size(axes) - 1)]
        down = lambda axes: [(i + 1, i) for i in range(lax.axis_size(axes) - 1)]
        return (
            lax.ppermute(right, lon, up(lon)),
            lax.ppermute(left, lon, down(lon)),
            lax.ppermute(mid, depth, up(depth)),
            lax.ppermute(mid, depth, down(depth)),
        )

    def pinned(*arrays):
        return tuple(pltpu.with_memory_space_constraint(a, VMEM) for a in arrays)

    packed = call(pack_kernel, pieces(ROWS), [spec()] * 2, nbytes=8 * ROWS * width)(probes, coords)
    halo = exchange(*packed)
    part, high, low = call(
        phi_own_kernel,
        (f32(TD, PROBES, TILE), *kept),
        [spec(SMEM)] + [spec()] * 3,
        scratch=[
            *lists,
            pltpu.VMEM((TD, FIRST, TILE), jnp.float32),
            pltpu.VMEM((TD, TILE, FIRST), jnp.float32),
            pltpu.VMEM((TD, 2 * PROBES, TILE), jnp.bfloat16),
        ],
        flops=pair_flops,
        nbytes=1 << 20,
    )(pairs, *packed)
    *image, high, low = call(
        phi_halo_kernel,
        (*pieces(PROBES), *kept),
        [spec(SMEM)] * 2 + [spec()] * 10,
        scratch=[
            *lists,
            pltpu.VMEM((TD, FIRST, TILE), jnp.float32),
            pltpu.VMEM((HALO, TILE, FIRST), jnp.float32),
            pltpu.VMEM((HALO, 2 * PROBES, TILE), jnp.bfloat16),
            pltpu.VMEM((TD, PROBES, TILE), jnp.float32),
        ],
        aliases={10: 3, 11: 4},
        flops=pair_flops,
        nbytes=1 << 20,
    )(pairs, scales, *packed, *halo, part, *pinned(high, low))
    halo = exchange(*image)
    part = call(
        own_kernel,
        f32(TD, PROBES, TILE),
        [spec(SMEM)] + [spec()] * 5,
        scratch=[*lists, pltpu.VMEM((TD, 2 * PROBES, TILE), jnp.bfloat16)],
        flops=pair_flops // 2,
        nbytes=1 << 20,
    )(pairs, *image, *pinned(high, low))
    far_image, dots = call(
        halo_kernel,
        (f32(PROBES, width), f32(lax.axis_size(("core", "z")), 128)),
        [spec(SMEM)] * 2 + [spec()] * 11,
        scratch=[
            *lists,
            pltpu.VMEM((HALO, 2 * PROBES, TILE), jnp.bfloat16),
            pltpu.VMEM((TD, PROBES, TILE), jnp.float32),
        ],
        flops=pair_flops // 2,
        nbytes=1 << 20,
    )(pairs, scales, probes, *image, *halo, part, *pinned(high, low))

    def swap(rows, axes):
        return lax.all_to_all(rows[:, None, :], axes, 0, 0, tiled=True)[:, 0, :]

    rows = swap(dots, ("core", "z"))
    rows = call(pass_kernel, f32(lax.axis_size(("y", "x")), 128), [spec()])(rows)
    rows = swap(rows, ("y", "x"))
    return call(final_kernel, (f32(PROBES, width),) * 2, [spec(), spec(SMEM)] + [spec()] * 5)(
        rows, scales, probes, *image, far_image
    )


def solution(mesh):
    shape = mesh.devices.shape
    cut = Mesh(mesh.devices.reshape(shape[0] // 2, 2, 4, shape[1] // 4), ("y", "core", "x", "z"))
    whole = ("y", "core", "x", "z")
    return jax.shard_map(
        body,
        mesh=cut,
        in_specs=(P(None, whole), P(None, whole), P(None, whole), P()),
        out_specs=(P(None, whole), P(None, whole)),
        check_vma=False,
    )
```

time: 509 us -> 129 us (0.25)
  blocking collectives: 307 us -> 37.1 us
  matrix products: 114 us -> 0 us
  Pallas kernels: 0 us -> 61.1 us
  local copies, waits for them, and re-layouts: 33.7 us -> 3.01 us
  waiting for transfers between devices: 15.7 us -> 0.03 us
  other arithmetic: 11.7 us -> 0 us
    psum x3 -> x0, blocking collectives: 307 us -> none  [the longest x2 205 us: squares_total(): return lax.psum(inner_product(residual, residual), ('depth', 'lon'))]
    dot_general x28 -> x0, matrix products: 114 us -> none  [the longest x14 107 us: add_block(): jnp.einsum('pij,cpj->cpi', weights, far_dir, precision=lax.Precision.HIGH...]
    pallas_call x0 -> x7, Pallas kernels: none -> 61.1 us  [the longest x1 18.5 us: body(): call(phi_halo_kernel, (*pieces(PROBES), *kept), [spec(SMEM)] * 2 + [spec(...]
    all_to_all x0 -> x2, blocking collectives: none -> 37.1 us  [swap(): return lax.all_to_all(rows[:, None, :], axes, 0, 0, tiled=True)[:, 0, :]]
    gather x42 -> x0, local copies, waits for them, and re-layouts: 24.5 us -> none  [the longest x14 8.3 us: add_block(): far_pts = jnp.take(ext_pts, far_rows, axis=1)]
    ppermute x8, waiting for transfers between devices: 15.7 us -> 0.03 us  [the longest x2 0.01 us: exchange(): lax.ppermute(left, lon, down(lon))]
    reduce_sum x5 -> x0, other arithmetic: 5.22 us -> none  [the longest x4 4.59 us: inner_product(): return jnp.sum(first_arr * second_arr, axis=(1, 2))]
  transfers between devices with their start and end apart: 8 -> 8, of which waited for: 5 -> 0; matrix products, arithmetic and copies ran while one was open for 0% -> 0% of each run, Pallas kernels for 0% -> 22%
where the time goes in v1:
time: 129 us
  Pallas kernels  61.1 us (47%)
  blocking collectives  37.1 us (29%)
  starting transfers between devices  26.8 us (21%)
  local copies, waits for them, and re-layouts  3.01 us (2%)
    all_to_all x2, blocking collectives, swap(): return lax.all_to_all(rows[:, None, :], axes, 0, 0, tiled=True)[:, 0, :]  37.1 us
    pallas_call x1, Pallas kernels, body(): call(phi_halo_kernel, (*pieces(PROBES), *kept), [spec(SMEM)] * 2 + [spec(...  18.5 us
    pallas_call x1, Pallas kernels, body(): call(phi_own_kernel, (f32(TD, PROBES, TILE), *kept), [spec(SMEM)] + [spec...  17.5 us
    pallas_call x1, Pallas kernels, body(): call(halo_kernel, (f32(PROBES, width), f32(lax.axis_size(('core', 'z')),...  12.2 us
    pallas_call x1, Pallas kernels, body(): call(own_kernel, f32(TD, PROBES, TILE), [spec(SMEM)] + [spec()] * 5, scra...  11.4 us
    ppermute x2, starting transfers between devices, exchange(): lax.ppermute(mid, depth, down(depth))  10.7 us
    ppermute x2, starting transfers between devices, exchange(): lax.ppermute(right, lon, up(lon))  7.98 us
    ppermute x2, starting transfers between devices, exchange(): lax.ppermute(mid, depth, up(depth))  5.56 us
  transfers between devices with their start and end apart: 8, of which 0 were waited for; matrix products, arithmetic and copies ran while one was open for 0% of the time, Pallas kernels for 22%

profile of v1, /device:TPU:1, one launch (start us, length us, event | category | flops | bytes accessed | tf_op | source)
XLA Modules:
  0.0 128.9 jit_solution(18291638606585963208)
XLA Ops:
  0.6 0.0 copy-start
  0.6 0.9 copy-done
  1.5 0.0 copy-start.2
  1.5 0.8 copy-done.2
  2.3 8.8 %collective-permute-start.3 = (f32[24,1280]{1,0:T(8,128)S(1)}, f32[24,1280]{1,0:T(8,128)S(1)}, u32[]{:S(2)}, u32[]{:S(2)}) collective-permute-start(f32[24,1280]{1,0:T(8,128)S(1)} %get-tuple-element.16.mid), channel_id=1, source_target_pairs={{64,0},{128,64},{192,128},{256,192},{320,256},{384,320},{448,384},... | collective-permute-start | bytes 368648 | tf_op jit(solution)/shard_map/ppermute | solution.py:268
  11.1 1.9 %collective-permute-start.2 = (f32[24,1280]{1,0:T(8,128)S(1)}, f32[24,1280]{1,0:T(8,128)S(1)}, u32[]{:S(2)}, u32[]{:S(2)}) collective-permute-start(f32[24,1280]{1,0:T(8,128)S(1)} %get-tuple-element.16.mid), channel_id=1, source_target_pairs={{0,64},{64,128},{128,192},{192,256},{256,320},{320,384},{384,448},... | collective-permute-start | bytes 368648 | tf_op jit(solution)/shard_map/ppermute | solution.py:267
  13.1 1.3 %collective-permute-start.1 = (f32[24,512]{1,0:T(8,128)S(1)}, f32[24,512]{1,0:T(8,128)S(1)}, u32[]{:S(2)}, u32[]{:S(2)}) collective-permute-start(f32[24,512]{1,0:T(8,128)S(1)} %get-tuple-element.15.left), channel_id=1, source_target_pairs={{1,0},{2,1},{3,2},{4,3},{5,4},{6,5},{7,6},{8,7},{9,8},{10,9},{11,1... | collective-permute-start | bytes 147464 | tf_op jit(solution)/shard_map/ppermute | solution.py:266
  14.4 4.0 %collective-permute-start = (f32[24,512]{1,0:T(8,128)S(1)}, f32[24,512]{1,0:T(8,128)S(1)}, u32[]{:S(2)}, u32[]{:S(2)}) collective-permute-start(f32[24,512]{1,0:T(8,128)S(1)} %get-tuple-element.17.right), channel_id=1, source_target_pairs={{0,1},{1,2},{2,3},{3,4},{4,5},{5,6},{6,7},{7,8},{8,9},{9,10},{10,1... | collective-permute-start | bytes 147464 | tf_op jit(solution)/shard_map/ppermute | solution.py:265
  18.4 0.0 copy-start.3
  18.4 0.7 copy-done.3
  19.0 17.5 %shard_map.60 = (f32[9,16,256]{2,1,0:T(8,128)S(1)}, bf16[113,256,256]{2,1,0:T(8,128)(2,1)S(1)}, bf16[113,256,256]{2,1,0:T(8,128)(2,1)S(1)}) custom-call(s32[2,112]{1,0:T(2,128)S(1)} %copy-done.3, f32[24,512]{1,0:T(8,128)S(1)} %get-tuple-element.15.left, f32[24,1280]{1,0:T(8,128)S(1)} %get-tuple-element.16.mid, f32[24,512]{1,0:T(8,128)S(1)} %get-tuple-element.17.right), custom_call_target="tpu_custom_call" | custom-call | flops 146800640 | bytes 1048576 | tf_op jit(solution)/shard_map/pallas_call | solution.py:276
  36.5 0.0 collective-permute-done.1.from_right
  36.6 0.0 collective-permute-done.from_left
  36.6 0.0 collective-permute-done.3.above
  36.6 0.0 collective-permute-done.2.below
  36.6 0.0 copy-start.5
  36.6 0.6 copy-done.5
  37.2 0.0 copy-start.4
  37.3 18.5 %shard_map.61 = (f32[16,512]{1,0:T(8,128)S(1)}, f32[16,1280]{1,0:T(8,128)S(1)}, f32[16,512]{1,0:T(8,128)S(1)}, bf16[113,256,256]{2,1,0:T(8,128)(2,1)S(1)}, bf16[113,256,256]{2,1,0:T(8,128)(2,1)S(1)}) custom-call(s32[2,112]{1,0:T(2,128)S(1)} %copy-done.3, f32[2]{0:T(128)S(1)} %copy-done.5, ...), custom_call_target="tpu_custom_call", output_to_operand_aliasing={{3}: (10, {}), {4}: (11, {})} | custom-call | flops 146800640 | bytes 1048576 | tf_op jit(solution)/shard_map/pallas_call | solution.py:289
  55.8 1.9 %collective-permute-start.7 = (f32[16,1280]{1,0:T(8,128)S(1)}, f32[16,1280]{1,0:T(8,128)S(1)}, u32[]{:S(2)}, u32[]{:S(2)}) collective-permute-start(f32[16,1280]{1,0:T(8,128)S(1)} %get-tuple-element.22.mid), channel_id=1, source_target_pairs={{64,0},{128,64},{192,128},{256,192},{320,256},{384,320},{448,384},... | collective-permute-start | bytes 245768 | tf_op jit(solution)/shard_map/ppermute | solution.py:268
  57.7 3.6 %collective-permute-start.6 = (f32[16,1280]{1,0:T(8,128)S(1)}, f32[16,1280]{1,0:T(8,128)S(1)}, u32[]{:S(2)}, u32[]{:S(2)}) collective-permute-start(f32[16,1280]{1,0:T(8,128)S(1)} %get-tuple-element.22.mid), channel_id=1, source_target_pairs={{0,64},{64,128},{128,192},{192,256},{256,320},{320,384},{384,448},... | collective-permute-start | bytes 245768 | tf_op jit(solution)/shard_map/ppermute | solution.py:267
  61.3 1.3 %collective-permute-start.5 = (f32[16,512]{1,0:T(8,128)S(1)}, f32[16,512]{1,0:T(8,128)S(1)}, u32[]{:S(2)}, u32[]{:S(2)}) collective-permute-start(f32[16,512]{1,0:T(8,128)S(1)} %get-tuple-element.21.left), channel_id=1, source_target_pairs={{1,0},{2,1},{3,2},{4,3},{5,4},{6,5},{7,6},{8,7},{9,8},{10,9},{11,1... | collective-permute-start | bytes 98312 | tf_op jit(solution)/shard_map/ppermute | solution.py:266
  62.6 4.0 %collective-permute-start.4 = (f32[16,512]{1,0:T(8,128)S(1)}, f32[16,512]{1,0:T(8,128)S(1)}, u32[]{:S(2)}, u32[]{:S(2)}) collective-permute-start(f32[16,512]{1,0:T(8,128)S(1)} %get-tuple-element.23.right), channel_id=1, source_target_pairs={{0,1},{1,2},{2,3},{3,4},{4,5},{5,6},{6,7},{7,8},{8,9},{9,10},{10,1... | collective-permute-start | bytes 98312 | tf_op jit(solution)/shard_map/ppermute | solution.py:265
  66.6 0.0 copy-done.4
  66.7 0.0 copy-start.1
  66.7 0.0 copy-start.6
  66.7 11.4 %shard_map.62.part = f32[9,16,256]{2,1,0:T(8,128)S(1)} custom-call(s32[2,112]{1,0:T(2,128)S(1)} %copy-done.4, f32[16,512]{1,0:T(8,128)S(1)} %get-tuple-element.21.left, f32[16,1280]{1,0:T(8,128)S(1)} %get-tuple-element.22.mid, f32[16,512]{1,0:T(8,128)S(1)} %get-tuple-element.23.right, bf16[113,256,256]{2,1,0:T(8,128)(2,1)S(1)} %get-tuple-element.24.high, ...), custom_call_target="tpu_custom_call" | custom-call | flops 73400320 | bytes 1048576 | tf_op jit(solution)/shard_map/pallas_call | solution.py:305
  78.1 0.0 collective-permute-done.5.from_right
  78.1 0.0 collective-permute-done.4.from_left
  78.1 0.0 collective-permute-done.7.above
  78.1 0.0 collective-permute-done.6.below
  78.1 0.0 copy-done.1
  78.1 0.0 copy-done.6
  78.1 12.2 %shard_map.63 = (f32[16,2304]{1,0:T(8,128)S(1)}, f32[32,128]{1,0:T(8,128)S(1)}) custom-call(s32[2,112]{1,0:T(2,128)S(1)} %copy-done.4, f32[2]{0:T(128)S(1)} %copy-done.6, f32[16,2304]{1,0:T(8,128)S(1)} %copy-done.1, f32[16,512]{1,0:T(8,128)S(1)} %get-tuple-element.21.left, f32[16,1280]{1,0:T(8,128)S(1)} %get-tuple-element.22.mid, ...), custom_call_target="tpu_custom_call" | custom-call | flops 73400320 | bytes 1048576 | tf_op jit(solution)/shard_map/pallas_call | solution.py:313
  90.4 20.8 %all_to_all.10 = f32[32,1,128]{2,1,0:T(1,128)S(1)} all-to-all(f32[32,1,128]{2,1,0:T(1,128)S(1)} %bitcast.11), channel_id=1, replica_groups=mesh['y'=4,'core'=2,'x'=4,'z'=16] {'core','z'}, dimensions={0} | all-to-all | bytes 32768 | tf_op jit(solution)/shard_map/all_to_all | solution.py:327
  111.2 16.3 %all_to_all.11 = f32[16,1,128]{2,1,0:T(1,128)S(1)} all-to-all(f32[16,1,128]{2,1,0:T(1,128)S(1)} %bitcast.10), channel_id=1, replica_groups=mesh['y'=4,'core'=2,'x'=4,'z'=16] {'y','x'}, dimensions={0} | all-to-all | bytes 16384 | tf_op jit(solution)/shard_map/all_to_all | solution.py:327
  127.5 1.4 %shard_map.65 = (f32[16,2304]{1,0:T(8,128)}, f32[16,2304]{1,0:T(8,128)}) custom-call(f32[16,128]{1,0:T(8,128)S(1)} %bitcast.9, f32[2]{0:T(128)S(1)} %copy-done.6, f32[16,2304]{1,0:T(8,128)S(1)} %copy-done.1, f32[16,512]{1,0:T(8,128)S(1)} %get-tuple-element.21.left, f32[16,1280]{1,0:T(8,128)S(1)} %get-tuple-element.22.mid, ...), custom_call_target="tpu_custom_call" | custom-call | tf_op jit(solution)/shard_map/pallas_call | solution.py:332
  (2 shorter events, 0.0 us)
Async XLA Ops:
  0.6 0.9 copy-start
  1.5 0.8 copy-start.2
  2.3 34.2 %collective-permute-start.3 = (f32[24,1280]{1,0:T(8,128)S(1)}, f32[24,1280]{1,0:T(8,128)S(1)}, u32[]{:S(2)}, u32[]{:S(2)}) collective-permute-start(f32[24,1280]{1,0:T(8,128)S(1)} %get-tuple-element.16.mid), channel_id=1, source_target_pairs={{64,0},{128,64},{192,128},{256,192},{320,256},{384,320},{448,384},... | collective-permute-start | bytes 368648 | tf_op jit(solution)/shard_map/ppermute | solution.py:268
  11.1 25.5 %collective-permute-start.2 = (f32[24,1280]{1,0:T(8,128)S(1)}, f32[24,1280]{1,0:T(8,128)S(1)}, u32[]{:S(2)}, u32[]{:S(2)}) collective-permute-start(f32[24,1280]{1,0:T(8,128)S(1)} %get-tuple-element.16.mid), channel_id=1, source_target_pairs={{0,64},{64,128},{128,192},{192,256},{256,320},{320,384},{384,448},... | collective-permute-start | bytes 368648 | tf_op jit(solution)/shard_map/ppermute | solution.py:267
  13.1 23.5 %collective-permute-start.1 = (f32[24,512]{1,0:T(8,128)S(1)}, f32[24,512]{1,0:T(8,128)S(1)}, u32[]{:S(2)}, u32[]{:S(2)}) collective-permute-start(f32[24,512]{1,0:T(8,128)S(1)} %get-tuple-element.15.left), channel_id=1, source_target_pairs={{1,0},{2,1},{3,2},{4,3},{5,4},{6,5},{7,6},{8,7},{9,8},{10,9},{11,1... | collective-permute-start | bytes 147464 | tf_op jit(solution)/shard_map/ppermute | solution.py:266
  14.4 22.2 %collective-permute-start = (f32[24,512]{1,0:T(8,128)S(1)}, f32[24,512]{1,0:T(8,128)S(1)}, u32[]{:S(2)}, u32[]{:S(2)}) collective-permute-start(f32[24,512]{1,0:T(8,128)S(1)} %get-tuple-element.17.right), channel_id=1, source_target_pairs={{0,1},{1,2},{2,3},{3,4},{4,5},{5,6},{6,7},{7,8},{8,9},{9,10},{10,1... | collective-permute-start | bytes 147464 | tf_op jit(solution)/shard_map/ppermute | solution.py:265
  18.4 0.7 copy-start.3
  36.6 0.7 copy-start.5
  37.2 29.4 %copy-start.4 = (s32[2,112]{1,0:T(2,128)S(1)}, s32[2,112]{1,0:T(2,128)}, u32[]{:S(2)}) copy-start(s32[2,112]{1,0:T(2,128)} %pairs.7) | copy-start | bytes 2692
  55.8 22.3 %collective-permute-start.7 = (f32[16,1280]{1,0:T(8,128)S(1)}, f32[16,1280]{1,0:T(8,128)S(1)}, u32[]{:S(2)}, u32[]{:S(2)}) collective-permute-start(f32[16,1280]{1,0:T(8,128)S(1)} %get-tuple-element.22.mid), channel_id=1, source_target_pairs={{64,0},{128,64},{192,128},{256,192},{320,256},{384,320},{448,384},... | collective-permute-start | bytes 245768 | tf_op jit(solution)/shard_map/ppermute | solution.py:268
  57.7 20.4 %collective-permute-start.6 = (f32[16,1280]{1,0:T(8,128)S(1)}, f32[16,1280]{1,0:T(8,128)S(1)}, u32[]{:S(2)}, u32[]{:S(2)}) collective-permute-start(f32[16,1280]{1,0:T(8,128)S(1)} %get-tuple-element.22.mid), channel_id=1, source_target_pairs={{0,64},{64,128},{128,192},{192,256},{256,320},{320,384},{384,448},... | collective-permute-start | bytes 245768 | tf_op jit(solution)/shard_map/ppermute | solution.py:267
  61.3 16.7 %collective-permute-start.5 = (f32[16,512]{1,0:T(8,128)S(1)}, f32[16,512]{1,0:T(8,128)S(1)}, u32[]{:S(2)}, u32[]{:S(2)}) collective-permute-start(f32[16,512]{1,0:T(8,128)S(1)} %get-tuple-element.21.left), channel_id=1, source_target_pairs={{1,0},{2,1},{3,2},{4,3},{5,4},{6,5},{7,6},{8,7},{9,8},{10,9},{11,1... | collective-permute-start | bytes 98312 | tf_op jit(solution)/shard_map/ppermute | solution.py:266
  62.6 15.4 %collective-permute-start.4 = (f32[16,512]{1,0:T(8,128)S(1)}, f32[16,512]{1,0:T(8,128)S(1)}, u32[]{:S(2)}, u32[]{:S(2)}) collective-permute-start(f32[16,512]{1,0:T(8,128)S(1)} %get-tuple-element.23.right), channel_id=1, source_target_pairs={{0,1},{1,2},{2,3},{3,4},{4,5},{5,6},{6,7},{7,8},{8,9},{9,10},{10,1... | collective-permute-start | bytes 98312 | tf_op jit(solution)/shard_map/ppermute | solution.py:265
  66.7 11.5 %copy-start.1 = (f32[16,2304]{1,0:T(8,128)S(1)}, f32[16,2304]{1,0:T(8,128)}, u32[]{:S(2)}) copy-start(f32[16,2304]{1,0:T(8,128)} %probes.5) | copy-start | bytes 442372
  66.7 11.5 %copy-start.6 = (f32[2]{0:T(128)S(1)}, f32[2]{0:T(128)}, u32[]{:S(2)}) copy-start(f32[2]{0:T(128)} %scales.5) | copy-start | bytes 28

commit v2 on v1

v2 whole, which is shorter than its diff:
```python
import jax
import jax.numpy as jnp
from jax import lax
from jax.experimental import pallas as pl
from jax.experimental.pallas import tpu as pltpu
from jax.sharding import Mesh, PartitionSpec as P

PROBES = 16
TILE = 256
TD = 9
BT = 2
MID = TD - 2 * BT
HALO = 2 * BT + 2 * MID
CHUNK = 32
GROUP = 4
ROWS = 24
FIRST = ROWS - PROBES
VMEM = pltpu.MemorySpace.VMEM
SMEM = pltpu.MemorySpace.SMEM
PARTS = ((0, BT), (BT, MID), (TD - BT, BT))


def call(kernel, out_shape, in_specs, scratch=(), aliases=None, flops=0, nbytes=0, limit=10):
    def place(out):
        return pl.BlockSpec(memory_space=getattr(out, "memory_space", VMEM))

    return pl.pallas_call(
        kernel,
        out_shape=out_shape,
        in_specs=in_specs,
        out_specs=jax.tree.map(place, out_shape),
        scratch_shapes=scratch,
        input_output_aliases=aliases or {},
        compiler_params=pltpu.CompilerParams(vmem_limit_bytes=limit << 20),
        cost_estimate=pl.CostEstimate(flops=flops, bytes_accessed=nbytes, transcendentals=0),
    )


def spec(space=VMEM):
    return pl.BlockSpec(memory_space=space)


def f32(*shape):
    return jax.ShapeDtypeStruct(shape, jnp.float32)


def pinned(space, *arrays):
    return tuple(pltpu.with_memory_space_constraint(a, space) for a in arrays)


def pack_kernel(probes, coords, pairs, scales, left, mid, right, pair_out, scale_out, sems):
    copies = [
        pltpu.make_async_copy(pairs, pair_out, sems.at[6]),
        pltpu.make_async_copy(scales, scale_out, sems.at[7]),
    ]
    for i, ((first, count), out) in enumerate(zip(PARTS, (left, mid, right))):
        cols = pl.ds(first * TILE, count * TILE)
        copies.append(pltpu.make_async_copy(probes.at[:, cols], out.at[FIRST:ROWS, :], sems.at[i]))
        copies.append(pltpu.make_async_copy(coords.at[:, cols], out.at[0:3, :], sems.at[3 + i]))
    for copy in copies:
        copy.start()
    for out in (left, mid, right):
        out[3:FIRST, :] = jnp.zeros((FIRST - 3, out.shape[1]), jnp.float32)
    for copy in copies:
        copy.wait()


def make_lists(pairs, rows, cols, counts):
    slots = pairs.shape[1]

    def close(taken, at):
        for i in range(GROUP):
            rows[at, taken + i] = TD
            cols[at, taken + i] = 0
        return (taken + GROUP - 1) // GROUP * GROUP

    def step(j, taken):
        own, halo = taken
        row, code = pairs[0, j], pairs[1, j]
        used = row < TD
        local = used & (code < TD)
        other = used & (code >= TD)
        place = jnp.where(
            code < 2 * TD,
            code - (2 * TD - BT),
            jnp.where(
                code < 3 * TD,
                code - 2 * TD + BT,
                jnp.where(code < 4 * TD, code - 3 * TD + BT, code - 4 * TD + BT + MID),
            ),
        )
        rows[0, own] = row
        cols[0, own] = code
        rows[1, halo] = row
        cols[1, halo] = place
        return own + local.astype(jnp.int32), halo + other.astype(jnp.int32)

    own, halo = lax.fori_loop(0, slots, step, (0, 0), unroll=4)
    counts[0] = close(own, 0)
    counts[1] = close(halo, 1)


def split(values):
    high = values.astype(jnp.bfloat16)
    return high, (values - high.astype(jnp.float32)).astype(jnp.bfloat16)


def put_vectors(values, vecs, at):
    high, low = split(values)
    vecs[at, 0:PROBES, :] = high
    vecs[at, PROBES:, :] = low


def evaluate(near, far, slot, high, low):
    for first in range(0, TILE, CHUNK):
        rows = pl.ds(first, CHUNK)
        for half in range(0, TILE, 128):
            lanes = pl.ds(half, 128)
            dx = near[0, rows, :] - far[0:1, lanes]
            dy = near[1, rows, :] - far[1:2, lanes]
            dz = near[2, rows, :] - far[2:3, lanes]
            dist_sq = dx * dx + dy * dy + dz * dz
            radius = dist_sq * lax.rsqrt(jnp.maximum(dist_sq, 1e-30))
            inside = jnp.maximum(1.0 - radius, 0.0)
            square = inside * inside
            phi = (square * square) * (1.25 - inside)
            top, rest = split(phi)
            high[slot, rows, lanes] = top
            low[slot, rows, lanes] = rest


def dot(vectors, matrix):
    return lax.dot_general(
        vectors, matrix, (((1,), (1,)), ((), ())), preferred_element_type=jnp.float32
    )


def multiply(vecs, source, slot, high, low):
    both = dot(vecs[source], high[slot])
    rest = dot(vecs[source, 0:PROBES, :], low[slot])
    return both[0:PROBES] + both[PROBES:] + rest


def add_group(first, base, rows, cols, vecs, total, high, low):
    sums = [
        (rows[first + i], multiply(vecs, cols[first + i], base + first + i, high, low))
        for i in range(GROUP)
    ]
    for row, value in sums:
        total[row] += value


def first_sweep(base, taken, rows, cols, near, far, vecs, total, high, low):
    def phi(first):
        for i in range(GROUP):
            evaluate(near.at[rows[first + i]], far.at[cols[first + i]], base + first + i, high, low)

    @pl.when(taken > 0)
    def _():
        phi(0)

        def step(k, carry):
            add_group(k * GROUP - GROUP, base, rows, cols, vecs, total, high, low)
            phi(k * GROUP)
            return carry

        lax.fori_loop(1, taken // GROUP, step, 0)
        add_group(taken - GROUP, base, rows, cols, vecs, total, high, low)


def second_sweep(base, taken, rows, cols, vecs, total, high, low):
    def step(k, carry):
        add_group(k * GROUP, base, rows, cols, vecs, total, high, low)
        return carry

    lax.fori_loop(0, taken // GROUP, step, 0)


def own_blocks(refs):
    for (first, count), ref in zip(PARTS, refs):
        for t in range(count):
            yield first + t, ref, pl.ds(t * TILE, TILE)


def halo_blocks(from_left, from_right, below, above):
    at = 0
    for ref, count in ((from_left, BT), (from_right, BT), (below, MID), (above, MID)):
        for t in range(count):
            yield at, ref, pl.ds(t * TILE, TILE)
            at += 1


def phi_own_kernel(
    pairs, left, mid, right, total, high, low, near, rows, cols, counts, far, vecs
):
    make_lists(pairs, rows, cols, counts)
    for t, ref, at in own_blocks((left, mid, right)):
        points = ref[0:FIRST, at]
        far[t] = points
        columns = points.T
        for i in range(3):
            near[t, i] = jnp.broadcast_to(columns[:, i : i + 1], (TILE, 128))
        put_vectors(ref[FIRST:ROWS, at], vecs, t)
    near[TD] = jnp.zeros((3, TILE, 128), jnp.float32)
    total[...] = jnp.zeros_like(total)
    first_sweep(0, counts[0], rows.at[0], cols.at[0], near, far, vecs, total, high, low)


def phi_halo_kernel(
    rows, cols, counts, scales, left, mid, right, from_left, from_right, below, above, part, near, high_in, low_in,
    p_left, p_mid, p_right, high, low, far, vecs, total,
):
    for t, ref, at in halo_blocks(from_left, from_right, below, above):
        far[t] = ref[0:FIRST, at]
        put_vectors(ref[FIRST:ROWS, at], vecs, t)
    total[...] = part[...]
    first_sweep(counts[0], counts[1], rows.at[1], cols.at[1], near, far, vecs, total, high, low)
    outs = {}
    for t, ref, at in own_blocks((p_left, p_mid, p_right)):
        outs[t] = (ref, at)
    for t, ref, at in own_blocks((left, mid, right)):
        out, place = outs[t]
        out[:, place] = scales[0] * (4.0 * total[t] - ref[FIRST:ROWS, at])


def own_kernel(rows, cols, counts, left, mid, right, high, low, total, vecs):
    for t, ref, at in own_blocks((left, mid, right)):
        put_vectors(ref[:, at], vecs, t)
    total[...] = jnp.zeros_like(total)
    second_sweep(0, counts[0], rows.at[0], cols.at[0], vecs, total, high, low)


def halo_kernel(
    rows, cols, counts, scales, r_left, r_mid, r_right, left, mid, right,
    from_left, from_right, below, above, part, high, low, image, dots, vecs, total,
):
    for t, ref, at in halo_blocks(from_left, from_right, below, above):
        put_vectors(ref[:, at], vecs, t)
    total[...] = part[...]
    second_sweep(counts[0], counts[1], rows.at[1], cols.at[1], vecs, total, high, low)
    probes = {t: ref[FIRST:ROWS, at] for t, ref, at in own_blocks((r_left, r_mid, r_right))}
    sums = [jnp.zeros((PROBES, TILE), jnp.float32) for _ in range(5)]
    for t, ref, at in own_blocks((left, mid, right)):
        p = ref[:, at]
        u = scales[0] * (4.0 * total[t] - p)
        r = probes[t]
        image[:, pl.ds(t * TILE, TILE)] = u
        for i, (one, other) in enumerate(((r, r), (r, p), (p, p), (r, u), (p, u))):
            sums[i] = sums[i] + one * other
    lane = lax.broadcasted_iota(jnp.int32, (PROBES, 128), 1)
    probe = lax.broadcasted_iota(jnp.int32, (PROBES, 128), 0)
    line = jnp.zeros((PROBES, 128), jnp.float32)
    for i, value in enumerate(sums):
        line = line + jnp.where(lane == i * PROBES + probe, jnp.sum(value, axis=1, keepdims=True), 0.0)
    dots[...] = jnp.broadcast_to(jnp.sum(line, axis=0, keepdims=True), dots.shape)


def pass_kernel(gathered, out):
    out[...] = jnp.broadcast_to(jnp.sum(gathered[...], axis=0, keepdims=True), out.shape)


def final_kernel(
    gathered, scales, r_left, r_mid, r_right, left, mid, right, image, solution, residual
):
    line = jnp.sum(gathered[...], axis=0, keepdims=True)
    lane = lax.broadcasted_iota(jnp.int32, (PROBES, 128), 1)
    probe = lax.broadcasted_iota(jnp.int32, (PROBES, 128), 0)
    spread = jnp.broadcast_to(line, (PROBES, 128))
    rr, rp, pp, ru, pu = [
        jnp.sum(jnp.where(lane == i * PROBES + probe, spread, 0.0), axis=1, keepdims=True)
        for i in range(5)
    ]
    shift = scales[0] + scales[1]
    first = rr / (shift * rr + rp)
    ratio = rp / rr
    norm = first * first * (pp - rp * ratio)
    turn = norm / rr
    keep = first * ratio + turn
    curve = (
        shift * (norm + turn * norm) + keep * keep * rp - keep * first * (ru + pp) + first * first * pu
    )
    second = norm / curve
    own_r = first + second * keep
    own_p = second * first
    res_r = first * ratio - second * shift * keep
    res_p = second * (shift * first - keep) - first
    res_u = second * first
    probes = {t: ref[FIRST:ROWS, at] for t, ref, at in own_blocks((r_left, r_mid, r_right))}
    for t, ref, at in own_blocks((left, mid, right)):
        cols = pl.ds(t * TILE, TILE)
        r, p = probes[t], ref[:, at]
        solution[:, cols] = own_r * r - own_p * p
        residual[:, cols] = res_r * r + res_p * p + res_u * image[:, cols]


def exchange(left, mid, right):
    lon = ("x", "z")
    depth = ("y", "core")
    up = lambda axes: [(i, i + 1) for i in range(lax.axis_size(axes) - 1)]
    down = lambda axes: [(i + 1, i) for i in range(lax.axis_size(axes) - 1)]
    return (
        lax.ppermute(right, lon, up(lon)),
        lax.ppermute(left, lon, down(lon)),
        lax.ppermute(mid, depth, up(depth)),
        lax.ppermute(mid, depth, down(depth)),
    )


def sweeps(probes, coords, pairs, scales, first_exchange, second_exchange, copies):
    slots = pairs.shape[1]
    width = probes.shape[1]
    pair_flops = 40 * TILE * TILE * slots // 2
    stored = (slots + 2 * GROUP, TILE, TILE)
    kept = (pltpu.VMEM(stored, jnp.bfloat16), pltpu.VMEM(stored, jnp.bfloat16))
    lists = (
        pltpu.SMEM((2, slots + GROUP), jnp.int32),
        pltpu.SMEM((2, slots + GROUP), jnp.int32),
        pltpu.SMEM((2,), jnp.int32),
    )
    pieces = lambda rows: tuple(f32(rows, count * TILE) for _, count in PARTS)
    total = (TD + 1, PROBES, TILE)

    *packed, pairs, scales = call(
        pack_kernel,
        (*pieces(ROWS), pltpu.SMEM(pairs.shape, jnp.int32), pltpu.SMEM(scales.shape, jnp.float32)),
        [spec(pl.ANY)] * 4,
        scratch=[pltpu.SemaphoreType.DMA((8,))],
        nbytes=8 * ROWS * width,
    )(*pinned(pltpu.MemorySpace.HBM, probes, coords, pairs, scales))
    halo = first_exchange(*packed)
    part, high, low, near, *lists = call(
        phi_own_kernel,
        (f32(*total), *kept, pltpu.VMEM((TD + 1, 3, TILE, 128), jnp.float32), *lists),
        [spec(SMEM)] + [spec()] * 3,
        scratch=[
            pltpu.VMEM((TD, FIRST, TILE), jnp.float32),
            pltpu.VMEM((TD, 2 * PROBES, TILE), jnp.bfloat16),
        ],
        flops=pair_flops,
        nbytes=1 << 20,
    )(*pinned(SMEM, pairs), *packed)
    lists = pinned(SMEM, *lists)
    (scales,) = pinned(SMEM, scales)
    *image, high, low = call(
        phi_halo_kernel,
        (*pieces(PROBES), *kept),
        [spec(SMEM)] * 4 + [spec()] * 11,
        scratch=[
            pltpu.VMEM((HALO, FIRST, TILE), jnp.float32),
            pltpu.VMEM((HALO, 2 * PROBES, TILE), jnp.bfloat16),
            pltpu.VMEM(total, jnp.float32),
        ],
        aliases={13: 3, 14: 4},
        flops=pair_flops,
        nbytes=1 << 20,
    )(*lists, scales, *packed, *halo, part, *pinned(VMEM, near, high, low))
    halo = second_exchange(*image)
    part = call(
        own_kernel,
        f32(*total),
        [spec(SMEM)] * 3 + [spec()] * 5,
        scratch=[pltpu.VMEM((TD, 2 * PROBES, TILE), jnp.bfloat16)],
        flops=pair_flops // 2,
        nbytes=1 << 20,
    )(*lists, *image, *pinned(VMEM, high, low))
    far_image, dots = call(
        halo_kernel,
        (f32(PROBES, width), f32(copies, 128)),
        [spec(SMEM)] * 4 + [spec()] * 13,
        scratch=[
            pltpu.VMEM((HALO, 2 * PROBES, TILE), jnp.bfloat16),
            pltpu.VMEM(total, jnp.float32),
        ],
        flops=pair_flops // 2,
        nbytes=1 << 20,
    )(*lists, scales, *packed, *image, *halo, part, *pinned(VMEM, high, low))
    return scales, packed, image, far_image, dots


def body(probes, coords, pairs, scales):
    scales, packed, image, far_image, dots = sweeps(
        probes, coords, pairs, scales, exchange, exchange, lax.axis_size(("core", "z"))
    )

    def swap(rows, axes):
        return lax.all_to_all(rows[:, None, :], axes, 0, 0, tiled=True)[:, 0, :]

    rows = swap(dots, ("core", "z"))
    rows = call(pass_kernel, f32(lax.axis_size(("y", "x")), 128), [spec()])(rows)
    rows = swap(rows, ("y", "x"))
    return call(final_kernel, (f32(*probes.shape),) * 2, [spec(), spec(SMEM)] + [spec()] * 7)(
        rows, scales, *packed, *image, far_image
    )


def solution(mesh):
    shape = mesh.devices.shape
    cut = Mesh(mesh.devices.reshape(shape[0] // 2, 2, 4, shape[1] // 4), ("y", "core", "x", "z"))
    whole = ("y", "core", "x", "z")
    return jax.shard_map(
        body,
        mesh=cut,
        in_specs=(P(None, whole), P(None, whole), P(None, whole), P()),
        out_specs=(P(None, whole), P(None, whole)),
        check_vma=False,
    )
```

time: 129 us -> 106 us (0.82)
  Pallas kernels: 61.1 us -> 41.1 us
  local copies, waits for them, and re-layouts: 3.01 us -> 0 us
    pallas_call x6, Pallas kernels: 61.1 us -> 41.1 us  [the longest x1 14.9 us: sweeps(): call(phi_own_kernel, (f32(*total), *kept, pltpu.VMEM((TD + 1, 3, TILE, 12...]
    unnamed x14 -> x0, local copies, waits for them, and re-layouts: 3.01 us -> none
  transfers between devices with their start and end apart: 8 -> 8, of which waited for: 0 -> 0; matrix products, arithmetic and copies ran while one was open for 0% -> 0% of each run, Pallas kernels for 22% -> 20%
where the time goes in v2:
time: 106 us; the launch traced here: 105 us
  Pallas kernels  41.1 us (39%)
  blocking collectives  36.6 us (35%)
  starting transfers between devices  26.8 us (25%)
    all_to_all x2, blocking collectives, swap(): return lax.all_to_all(rows[:, None, :], axes, 0, 0, tiled=True)[:, 0, :]  36.6 us
    pallas_call x1, Pallas kernels, sweeps(): call(phi_own_kernel, (f32(*total), *kept, pltpu.VMEM((TD + 1, 3, TILE, 12...  14.9 us
    pallas_call x1, Pallas kernels, sweeps(): call(phi_halo_kernel, (*pieces(PROBES), *kept), [spec(SMEM)] * 4 + [spec(...  12.7 us
    ppermute x2, starting transfers between devices, exchange(): lax.ppermute(mid, depth, down(depth))  10.7 us
    ppermute x2, starting transfers between devices, exchange(): lax.ppermute(right, lon, up(lon))  7.98 us
    pallas_call x1, Pallas kernels, sweeps(): call(halo_kernel, (f32(PROBES, width), f32(copies, 128)), [spec(SMEM)] *...  5.93 us
    pallas_call x1, Pallas kernels, sweeps(): call(own_kernel, f32(*total), [spec(SMEM)] * 3 + [spec()] * 5, scratch=[p...  5.73 us
    ppermute x2, starting transfers between devices, exchange(): lax.ppermute(mid, depth, up(depth))  5.56 us
  transfers between devices with their start and end apart: 8, of which 0 were waited for; matrix products, arithmetic and copies ran while one was open for 0% of the time, Pallas kernels for 20%

profile of v2, /device:TPU:1, one launch (start us, length us, event | category | flops | bytes accessed | tf_op | source)
XLA Modules:
  0.0 105.3 jit_solution(13642096697722773068)
XLA Ops:
  0.6 1.0 shard_map.59
  1.6 8.8 %collective-permute-start.3 = (f32[24,1280]{1,0:T(8,128)S(1)}, f32[24,1280]{1,0:T(8,128)S(1)}, u32[]{:S(2)}, u32[]{:S(2)}) collective-permute-start(f32[24,1280]{1,0:T(8,128)S(1)} %get-tuple-element.23.mid.r_mid), channel_id=1, source_target_pairs={{64,0},{128,64},{192,128},{256,192},{320,256},{384,320},{448,384},... | collective-permute-start | bytes 368648 | tf_op jit(solution)/shard_map/ppermute | solution.py:305
  10.4 1.9 %collective-permute-start.2 = (f32[24,1280]{1,0:T(8,128)S(1)}, f32[24,1280]{1,0:T(8,128)S(1)}, u32[]{:S(2)}, u32[]{:S(2)}) collective-permute-start(f32[24,1280]{1,0:T(8,128)S(1)} %get-tuple-element.23.mid.r_mid), channel_id=1, source_target_pairs={{0,64},{64,128},{128,192},{192,256},{256,320},{320,384},{384,448},... | collective-permute-start | bytes 368648 | tf_op jit(solution)/shard_map/ppermute | solution.py:304
  12.4 1.3 %collective-permute-start.1 = (f32[24,512]{1,0:T(8,128)S(1)}, f32[24,512]{1,0:T(8,128)S(1)}, u32[]{:S(2)}, u32[]{:S(2)}) collective-permute-start(f32[24,512]{1,0:T(8,128)S(1)} %get-tuple-element.22.left.r_left), channel_id=1, source_target_pairs={{1,0},{2,1},{3,2},{4,3},{5,4},{6,5},{7,6},{8,7},{9,8},{10,9},{11,1... | collective-permute-start | bytes 147464 | tf_op jit(solution)/shard_map/ppermute | solution.py:303
  13.7 4.0 %collective-permute-start = (f32[24,512]{1,0:T(8,128)S(1)}, f32[24,512]{1,0:T(8,128)S(1)}, u32[]{:S(2)}, u32[]{:S(2)}) collective-permute-start(f32[24,512]{1,0:T(8,128)S(1)} %get-tuple-element.24.right.r_right), channel_id=1, source_target_pairs={{0,1},{1,2},{2,3},{3,4},{4,5},{5,6},{6,7},{7,8},{8,9},{9,10},{10,1... | collective-permute-start | bytes 147464 | tf_op jit(solution)/shard_map/ppermute | solution.py:302
  17.7 14.9 %shard_map.60 = (f32[10,16,256]{2,1,0:T(8,128)S(1)}, bf16[120,256,256]{2,1,0:T(8,128)(2,1)S(1)}, bf16[120,256,256]{2,1,0:T(8,128)(2,1)S(1)}, f32[10,3,256,128]{3...) custom-call(s32[2,112]{1,0:T(2,128)S(4)} %get-tuple-element.21.pairs, ...), custom_call_target="tpu_custom_call" | custom-call | flops 146800640 | bytes 1048576 | tf_op jit(solution)/shard_map/pallas_call | solution.py:331
  32.5 0.0 collective-permute-done.1.from_right
  32.5 0.0 collective-permute-done.from_left
  32.6 0.0 collective-permute-done.3.above
  32.6 0.0 collective-permute-done.2.below
  32.6 12.7 %shard_map.61 = (f32[16,512]{1,0:T(8,128)S(1)}, f32[16,1280]{1,0:T(8,128)S(1)}, f32[16,512]{1,0:T(8,128)S(1)}, bf16[120,256,256]{2,1,0:T(8,128)(2,1)S(1)}, bf16[120,256,256]{2,1,0:T(8,128)(2,1)S(1)}) custom-call(s32[2,116]{1,0:T(2,128)S(4)} %get-tuple-element.25.rows, ...), custom_call_target="tpu_custom_call", output_to_operand_aliasing={{3}: (13, {}), {4}: (14, {})} | custom-call | flops 146800640 | bytes 1048576 | tf_op jit(solution)/shard_map/pallas_call | solution.py:344
  45.3 1.9 %collective-permute-start.7 = (f32[16,1280]{1,0:T(8,128)S(1)}, f32[16,1280]{1,0:T(8,128)S(1)}, u32[]{:S(2)}, u32[]{:S(2)}) collective-permute-start(f32[16,1280]{1,0:T(8,128)S(1)} %get-tuple-element.34.mid), channel_id=1, source_target_pairs={{64,0},{128,64},{192,128},{256,192},{320,256},{384,320},{448,384},... | collective-permute-start | bytes 245768 | tf_op jit(solution)/shard_map/ppermute | solution.py:305
  47.2 3.6 %collective-permute-start.6 = (f32[16,1280]{1,0:T(8,128)S(1)}, f32[16,1280]{1,0:T(8,128)S(1)}, u32[]{:S(2)}, u32[]{:S(2)}) collective-permute-start(f32[16,1280]{1,0:T(8,128)S(1)} %get-tuple-element.34.mid), channel_id=1, source_target_pairs={{0,64},{64,128},{128,192},{192,256},{256,320},{320,384},{384,448},... | collective-permute-start | bytes 245768 | tf_op jit(solution)/shard_map/ppermute | solution.py:304
  50.9 1.3 %collective-permute-start.5 = (f32[16,512]{1,0:T(8,128)S(1)}, f32[16,512]{1,0:T(8,128)S(1)}, u32[]{:S(2)}, u32[]{:S(2)}) collective-permute-start(f32[16,512]{1,0:T(8,128)S(1)} %get-tuple-element.33.left), channel_id=1, source_target_pairs={{1,0},{2,1},{3,2},{4,3},{5,4},{6,5},{7,6},{8,7},{9,8},{10,9},{11,1... | collective-permute-start | bytes 98312 | tf_op jit(solution)/shard_map/ppermute | solution.py:303
  52.2 4.0 %collective-permute-start.4 = (f32[16,512]{1,0:T(8,128)S(1)}, f32[16,512]{1,0:T(8,128)S(1)}, u32[]{:S(2)}, u32[]{:S(2)}) collective-permute-start(f32[16,512]{1,0:T(8,128)S(1)} %get-tuple-element.35.right), channel_id=1, source_target_pairs={{0,1},{1,2},{2,3},{3,4},{4,5},{5,6},{6,7},{7,8},{8,9},{9,10},{10,1... | collective-permute-start | bytes 98312 | tf_op jit(solution)/shard_map/ppermute | solution.py:302
  56.2 5.7 %shard_map.62.part = f32[10,16,256]{2,1,0:T(8,128)S(1)} custom-call(s32[2,116]{1,0:T(2,128)S(4)} %get-tuple-element.25.rows, s32[2,116]{1,0:T(2,128)S(4)} %get-tuple-element.26.cols, s32[2]{0:T(128)S(4)} %get-tuple-element.27.counts, f32[16,512]{1,0:T(8,128)S(1)} %get-tuple-element.33.left, f32[16,1280]{1,0:T(8,128)S(1)} %get-tuple-element.34.mid, ...), custom_call_target="tpu_custom_call" | custom-call | flops 73400320 | bytes 1048576 | tf_op jit(solution)/shard_map/pallas_call | solution.py:358
  61.9 0.0 collective-permute-done.5.from_right
  61.9 0.0 collective-permute-done.4.from_left
  61.9 0.0 collective-permute-done.7.above
  61.9 0.0 collective-permute-done.6.below
  61.9 5.9 %shard_map.63 = (f32[16,2304]{1,0:T(8,128)S(1)}, f32[32,128]{1,0:T(8,128)S(1)}) custom-call(s32[2,116]{1,0:T(2,128)S(4)} %get-tuple-element.25.rows, s32[2,116]{1,0:T(2,128)S(4)} %get-tuple-element.26.cols, s32[2]{0:T(128)S(4)} %get-tuple-element.27.counts, f32[2]{0:T(128)S(4)} %get-tuple-element.28.scales, f32[24,512]{1,0:T(8,128)S(1)} %get-tuple-element.22.left.r_left, ...), custom_call_target="tpu_custom_call" | custom-call | flops 73400320 | bytes 1048576 | tf_op jit(solution)/shard_map/pallas_call | solution.py:366
  67.9 24.2 %all_to_all.10 = f32[32,1,128]{2,1,0:T(1,128)S(1)} all-to-all(f32[32,1,128]{2,1,0:T(1,128)S(1)} %bitcast.11), channel_id=1, replica_groups=mesh['y'=4,'core'=2,'x'=4,'z'=16] {'core','z'}, dimensions={0} | all-to-all | bytes 32768 | tf_op jit(solution)/shard_map/all_to_all | solution.py:386
  92.1 12.4 %all_to_all.11 = f32[16,1,128]{2,1,0:T(1,128)S(1)} all-to-all(f32[16,1,128]{2,1,0:T(1,128)S(1)} %bitcast.10), channel_id=1, replica_groups=mesh['y'=4,'core'=2,'x'=4,'z'=16] {'y','x'}, dimensions={0} | all-to-all | bytes 16384 | tf_op jit(solution)/shard_map/all_to_all | solution.py:386
  104.5 0.9 shard_map.65
  (1 shorter events, 0.0 us)
Async XLA Ops:
  1.6 30.9 %collective-permute-start.3 = (f32[24,1280]{1,0:T(8,128)S(1)}, f32[24,1280]{1,0:T(8,128)S(1)}, u32[]{:S(2)}, u32[]{:S(2)}) collective-permute-start(f32[24,1280]{1,0:T(8,128)S(1)} %get-tuple-element.23.mid.r_mid), channel_id=1, source_target_pairs={{64,0},{128,64},{192,128},{256,192},{320,256},{384,320},{448,384},... | collective-permute-start | bytes 368648 | tf_op jit(solution)/shard_map/ppermute | solution.py:305
  10.4 22.1 %collective-permute-start.2 = (f32[24,1280]{1,0:T(8,128)S(1)}, f32[24,1280]{1,0:T(8,128)S(1)}, u32[]{:S(2)}, u32[]{:S(2)}) collective-permute-start(f32[24,1280]{1,0:T(8,128)S(1)} %get-tuple-element.23.mid.r_mid), channel_id=1, source_target_pairs={{0,64},{64,128},{128,192},{192,256},{256,320},{320,384},{384,448},... | collective-permute-start | bytes 368648 | tf_op jit(solution)/shard_map/ppermute | solution.py:304
  12.4 20.2 %collective-permute-start.1 = (f32[24,512]{1,0:T(8,128)S(1)}, f32[24,512]{1,0:T(8,128)S(1)}, u32[]{:S(2)}, u32[]{:S(2)}) collective-permute-start(f32[24,512]{1,0:T(8,128)S(1)} %get-tuple-element.22.left.r_left), channel_id=1, source_target_pairs={{1,0},{2,1},{3,2},{4,3},{5,4},{6,5},{7,6},{8,7},{9,8},{10,9},{11,1... | collective-permute-start | bytes 147464 | tf_op jit(solution)/shard_map/ppermute | solution.py:303
  13.7 18.9 %collective-permute-start = (f32[24,512]{1,0:T(8,128)S(1)}, f32[24,512]{1,0:T(8,128)S(1)}, u32[]{:S(2)}, u32[]{:S(2)}) collective-permute-start(f32[24,512]{1,0:T(8,128)S(1)} %get-tuple-element.24.right.r_right), channel_id=1, source_target_pairs={{0,1},{1,2},{2,3},{3,4},{4,5},{5,6},{6,7},{7,8},{8,9},{9,10},{10,1... | collective-permute-start | bytes 147464 | tf_op jit(solution)/shard_map/ppermute | solution.py:302
  45.3 16.6 %collective-permute-start.7 = (f32[16,1280]{1,0:T(8,128)S(1)}, f32[16,1280]{1,0:T(8,128)S(1)}, u32[]{:S(2)}, u32[]{:S(2)}) collective-permute-start(f32[16,1280]{1,0:T(8,128)S(1)} %get-tuple-element.34.mid), channel_id=1, source_target_pairs={{64,0},{128,64},{192,128},{256,192},{320,256},{384,320},{448,384},... | collective-permute-start | bytes 245768 | tf_op jit(solution)/shard_map/ppermute | solution.py:305
  47.2 14.7 %collective-permute-start.6 = (f32[16,1280]{1,0:T(8,128)S(1)}, f32[16,1280]{1,0:T(8,128)S(1)}, u32[]{:S(2)}, u32[]{:S(2)}) collective-permute-start(f32[16,1280]{1,0:T(8,128)S(1)} %get-tuple-element.34.mid), channel_id=1, source_target_pairs={{0,64},{64,128},{128,192},{192,256},{256,320},{320,384},{384,448},... | collective-permute-start | bytes 245768 | tf_op jit(solution)/shard_map/ppermute | solution.py:304
  50.9 11.0 %collective-permute-start.5 = (f32[16,512]{1,0:T(8,128)S(1)}, f32[16,512]{1,0:T(8,128)S(1)}, u32[]{:S(2)}, u32[]{:S(2)}) collective-permute-start(f32[16,512]{1,0:T(8,128)S(1)} %get-tuple-element.33.left), channel_id=1, source_target_pairs={{1,0},{2,1},{3,2},{4,3},{5,4},{6,5},{7,6},{8,7},{9,8},{10,9},{11,1... | collective-permute-start | bytes 98312 | tf_op jit(solution)/shard_map/ppermute | solution.py:303
  52.2 9.7 %collective-permute-start.4 = (f32[16,512]{1,0:T(8,128)S(1)}, f32[16,512]{1,0:T(8,128)S(1)}, u32[]{:S(2)}, u32[]{:S(2)}) collective-permute-start(f32[16,512]{1,0:T(8,128)S(1)} %get-tuple-element.35.right), channel_id=1, source_target_pairs={{0,1},{1,2},{2,3},{3,4},{4,5},{5,6},{6,7},{7,8},{8,9},{9,10},{10,1... | collective-permute-start | bytes 98312 | tf_op jit(solution)/shard_map/ppermute | solution.py:302
